TPU v7x, 32 devices: a whole 2x2x4 slice. The times are simulated.
32 devices in a mesh: dp: 2 (over y), seq: 16 (over z, x, core).
Axes of the slice: x: 2, y: 2, z: 4, core: 2. Of those that a mesh axis runs over, the one named last changes fastest.
Arguments:
- tokens: bfloat16 [2, 8192, 1024], P('dp', 'seq'), may hold values from -50 to 50
- w_query: bfloat16 [1024, 1024], P(None, 'dp'), may hold values from -0.1875 to 0.1875
- w_key: bfloat16 [1024, 1024], P(None, 'dp'), may hold values from -0.1875 to 0.1875
- w_value: bfloat16 [1024, 1024], P(None, 'dp'), may hold values from -0.1875 to 0.1875
- w_out: bfloat16 [1024, 1024], P('dp'), may hold values from -0.1875 to 0.1875
- norm_gain: float32 [1024], replicated, may hold values from 0.1 to 1.9
Outputs:
- layer_out: bfloat16 [2, 8192, 1024], P('dp', 'seq')
All inputs are finite; a program needn't handle non-finite values.
Results may differ from a plain program's by a relative error of at most 0.017.
Values may be sent and summed in bfloat16 or wider, within the bound.
A program may use at most 128 MiB of HBM per device.

v0:
```python
import jax
import jax.numpy as jnp
from jax import lax
from jax.sharding import PartitionSpec as P

H = 8
DH = 128


def entering(value, axis, join, neutral):
    place = lax.axis_index(axis)
    gathered = lax.all_gather(value.astype(jnp.bfloat16), axis)
    state = jnp.zeros_like(value) + jnp.asarray(neutral, value.dtype)

    def one(lap, state):
        return join(state, lax.dynamic_index_in_dim(gathered, lap, 0, False).astype(value.dtype))

    return lax.fori_loop(0, place, one, state)


def inner_block(query_heads, key_heads, value_heads):
    length = query_heads.shape[1]
    block = min(length, 512)
    scores = jnp.einsum("hid,hjd->hij", query_heads, key_heads, preferred_element_type=jnp.float32)
    row_ids = jnp.arange(0, block)[:, None]
    col_ids = jnp.arange(block)[None, :]
    scores = jnp.where(col_ids <= row_ids, scores, 0.0).astype(jnp.bfloat16)
    pieces = jnp.einsum("hij,hje->hie", scores, value_heads, preferred_element_type=jnp.float32)
    return pieces


def add_states(earlier, later):
    return earlier + later


def key_value_state(key_heads, value_heads):
    return jnp.einsum("htd,hte->hde", key_heads, value_heads, preferred_element_type=jnp.float32)


def attend(query_heads, key_heads, value_heads, prior):
    within = inner_block(query_heads, key_heads, value_heads)
    carried = jnp.einsum(
        "htd,hde->hte", query_heads, prior.astype(jnp.bfloat16), preferred_element_type=jnp.float32
    )
    return within + carried


def body(tokens, w_query, w_key, w_value, w_out, norm_gain):
    rows = tokens[0]
    length = rows.shape[0]
    stacked = jnp.stack([w_query, w_key, w_value], axis=0)
    projected = jnp.einsum(
        "td,pdc->ptc",
        rows,
        lax.all_gather(stacked, "dp", axis=2, tiled=True),
        preferred_element_type=jnp.float32,
    ).astype(jnp.bfloat16)
    query = projected[0]
    key = projected[1]
    value = projected[2]
    query_heads = query.reshape(length, H, DH).transpose(1, 0, 2)
    key_heads = key.reshape(length, H, DH).transpose(1, 0, 2)
    value_heads = value.reshape(length, H, DH).transpose(1, 0, 2)
    local_state = key_value_state(key_heads, value_heads)
    empty_state = jnp.zeros((H, DH, DH), jnp.float32)
    prior = entering(local_state, "seq", add_states, empty_state)
    mixed_raw = attend(query_heads, key_heads, value_heads, prior)
    scale = lax.rsqrt(jnp.mean(mixed_raw * mixed_raw, axis=-1, keepdims=True) + 1e-05)
    normed = (mixed_raw * scale * norm_gain.reshape(H, 1, DH)).astype(jnp.bfloat16)
    normed = normed.transpose(1, 0, 2).reshape(length, H * DH)
    result = jnp.dot(
        normed, lax.all_gather(w_out, "dp", axis=0, tiled=True), preferred_element_type=jnp.float32
    )
    return result.astype(jnp.bfloat16)[None]


def solution(mesh):
    in_specs = (
        P("dp", "seq", None),
        P(None, "dp"),
        P(None, "dp"),
        P(None, "dp"),
        P("dp", None),
        P(),
    )
    out_specs = P("dp", "seq", None)
    return jax.shard_map(body, mesh=mesh, in_specs=in_specs, out_specs=out_specs, check_vma=False)
```

profile of v0, /device:TPU:0, one launch (start us, length us, event | category | flops | bytes accessed | tf_op | source)
XLA Modules:
  0.0 202.5 jit_solution(4533514288469171736)
XLA Ops:
  6.5 0.0 copy-start
  6.5 0.0 all-gather.5.cloned.1.call-start
  6.5 1.6 copy.13
  8.1 1.5 copy.14
  9.6 2.3 %copy.15 = bf16[1024,512]{0,1:T(8,128)(2,1)} copy(bf16[1024,512]{1,0:T(8,128)(2,1)} %param.11) | data formatting | bytes 2097152 | tf_op args[3]
  11.9 3.3 %pad_maximum_fusion = bf16[3,1024,512]{1,2,0:T(8,128)(2,1)} fusion(bf16[1,1024,512]{1,2,0:T(8,128)(2,1)} %bitcast.57, bf16[1,1024,512]{1,2,0:T(8,128)(2,1)S(1)} %bitcast.56, bf16[1,1024,512]{1,2,0:T(8,128)(2,1)S(1)} %bitcast.55), kind=kLoop, calls=%fused_computation.6 | loop fusion | flops 3145728 | bytes 6291456 | tf_op jit(solution)/shard_map/stack | solution.py:51
  15.2 0.0 all-gather.5.cloned.1.call-update
  15.2 0.0 all-gather.9.cloned.1.call-start
  15.2 83.2 %all-gather.5.cloned.1.call-done = bf16[3,1024,1024]{1,2,0:T(8,128)(2,1)} async-done(((bf16[3,1024,512]{1,2,0:T(8,128)(2,1)}), bf16[3,1024,1024]{1,2,0:T(8,128)(2,1)}) %all-gather.5.cloned.1.call-update) | async-done | bytes 6291472 | tf_op jit(solution)/shard_map/all_gather | solution.py:55
  98.4 0.0 copy-done
  98.4 6.5 %convert_bitcast_fusion = bf16[3,512,1024]{1,2,0:T(8,128)(2,1)S(1)} fusion(bf16[3,1024,1024]{1,2,0:T(8,128)(2,1)} %all-gather.5.cloned.1.call-done, bf16[1,512,1024]{2,1,0:T(8,128)(2,1)S(1)} %copy-done), kind=kOutput, calls=%fused_computation.7 | convolution fusion | flops 3222798336 | bytes 10485760 | tf_op jit(solution)/shard_map/td,pdc->ptc/dot_general | solution.py:52
  104.9 1.2 fusion.14
  106.1 0.0 copy-start.1
  106.1 1.1 copy-done.1
  107.1 1.2 convolution_convert_fusion.1
  108.3 0.0 all-gather.9.cloned.1.call-update
  108.3 0.0 all-gather.7.cloned.1.call-start
  108.4 0.7 all-gather.7.cloned.1.call-update
  109.1 0.1 iota_compare_fusion
  109.2 1.6 copy.16
  110.8 5.1 %fusion = f32[8,512,128]{1,2,0:T(8,128)} fusion(bf16[8,512,128]{1,2,0:T(8,128)(2,1)S(1)} %bitcast.50, pred[512,512]{1,0:T(8,128)(4,1)S(1)} %iota_compare_fusion, bf16[8,512,128]{1,2,0:T(8,128)(2,1)} %bitcast.52, bf16[512,8,128]{2,0,1:T(8,128)(2,1)S(1)} %copy.16), kind=kOutput, calls=%fused_computation.2 | convolution fusion | flops 1077936128 | bytes 5505024 | tf_op jit(solution)/shard_map/hij,hje->hie/dot_general | solution.py:28
  115.9 43.0 %all-gather.9.cloned.1.call-done = bf16[128,128,128]{2,1,0:T(8,128)(2,1)} async-done(((bf16[8,128,128]{2,1,0:T(8,128)(2,1)}), bf16[128,128,128]{2,1,0:T(8,128)(2,1)}) %all-gather.9.cloned.1.call-update) | async-done | bytes 4194320 | tf_op jit(solution)/shard_map/all_gather | solution.py:12
  159.0 0.0 copy-start.2
  159.0 2.1 %multiply_reduce_fusion = (f32[8,512]{1,0:T(8,128)S(1)}, f32[8,512,128]{1,2,0:T(8,128)S(1)}) fusion(f32[8,512,128]{1,2,0:T(8,128)} %fusion, f32[8,128,128]{2,1,0:T(8,128)S(1)} %get-tuple-element.28, bf16[512,8,128]{2,0,1:T(8,128)(2,1)S(1)} %copy.16), kind=kOutput, calls=%fused_computation.11 | convolution fusion | flops 135917568 | bytes 5783552 | tf_op jit(solution)/shard_map/htd,hde->hte/dot_general | solution.py:42
  161.1 0.0 copy-done.2
  161.1 0.3 fusion.6
  161.4 30.7 %all-gather.7.cloned.1.call-done = bf16[1024,1024]{1,0:T(8,128)(2,1)} async-done(((bf16[512,1024]{1,0:T(8,128)(2,1)}), bf16[1024,1024]{1,0:T(8,128)(2,1)}) %all-gather.7.cloned.1.call-update) | async-done | bytes 2097168 | tf_op jit(solution)/shard_map/all_gather | solution.py:72
  192.1 3.8 %fusion.7 = bf16[1,512,1024]{2,1,0:T(8,128)(2,1)} fusion(bf16[512,1024]{0,1:T(8,128)(2,1)S(1)} %bitcast.54, bf16[1024,1024]{1,0:T(8,128)(2,1)} %all-gather.7.cloned.1.call-done), kind=kOutput, calls=%fused_computation.14 | convolution fusion | flops 1074266112 | bytes 4194304 | tf_op jit(solution)/shard_map/dot_general | solution.py:71
  (3 shorter events, 0.1 us)
Async XLA Ops:
  6.5 91.9 %copy-start = (bf16[1,512,1024]{2,1,0:T(8,128)(2,1)S(1)}, bf16[1,512,1024]{2,1,0:T(8,128)(2,1)}, u32[]{:S(2)}) copy-start(bf16[1,512,1024]{2,1,0:T(8,128)(2,1)} %param.8) | copy-start | bytes 3145732
  6.5 91.9 %all-gather.5.cloned.1.call-start = ((), (), s32[]{:S(2)}) async-start(), calls=%async_computation | async-start | bytes 9437184 | tf_op jit(solution)/shard_map/all_gather | solution.py:55
  15.2 143.7 %all-gather.9.cloned.1.call-start = ((), (), s32[]{:S(2)}) async-start(), calls=%async_computation.2 | async-start | bytes 4456448 | tf_op jit(solution)/shard_map/all_gather | solution.py:12
  106.1 1.1 copy-start.1
  108.3 83.8 %all-gather.7.cloned.1.call-start = ((), (), s32[]{:S(2)}) async-start(), calls=%async_computation.1 | async-start | bytes 3145728 | tf_op jit(solution)/shard_map/all_gather | solution.py:72
  159.0 2.1 %copy-start.2 = (f32[1024]{0:T(1024)S(1)}, f32[1024]{0:T(1024)}, u32[]{:S(2)}) copy-start(f32[1024]{0:T(1024)} %param.13) | copy-start | bytes 12292
Sparse Core Ops, SparseCore 0:
  15.3 83.0 all-gather.4
  108.5 50.3 all-gather.8
  160.5 31.6 all-gather.6
where the time goes:
time: 203 us; the launch traced here: 202 us
  waiting for transfers between devices  158 us (78%)
  matrix products  18.7 us (9%)
  between operations  13.2 us (7%)
  local copies, waits for them, and re-layouts  9.22 us (5%)
  other arithmetic  3.68 us (2%)
    all_gather x1, waiting for transfers between devices, body(): lax.all_gather(stacked, 'dp', axis=2, tiled=True)  83.2 us
    all_gather x1, waiting for transfers between devices, entering(): gathered = lax.all_gather(value.astype(jnp.bfloat16), axis)  43 us
    all_gather x1, waiting for transfers between devices, body(): lax.all_gather(w_out, 'dp', axis=0, tiled=True)  30.7 us
    dot_general x1, matrix products, body(): jnp.einsum('td,pdc->ptc', rows, lax.all_gather(stacked, 'dp', axis=2, til...  6.49 us
    unnamed x9, local copies, waits for them, and re-layouts  6.4 us
    dot_general x1, matrix products, inner_block(): jnp.einsum('hij,hje->hie', scores, value_heads, preferred_element_type=jn...  5.12 us
  transfers between devices with their start and end apart: 3, of which 3 were waited for; matrix products, arithmetic and copies ran while one was open for 5% of the time, Pallas kernels for 0%

commit v1 on v0

v1 whole, which is shorter than its diff:
```python
import functools

import jax
import jax.numpy as jnp
from jax import lax
from jax.experimental import pallas as pl
from jax.experimental.pallas import tpu as pltpu
from jax.sharding import PartitionSpec as P

H = 8
DH = 128
GROUP = 4
MESH = pl.DeviceIdType.MESH
F32 = jnp.float32
BF16 = jnp.bfloat16


class Scan:
    def __init__(self, seq, steps, state, total, before, send, recv, prior, fin, send_sem, recv_sem):
        self.seq, self.steps = seq, steps
        self.state, self.total, self.before = state, total, before
        self.send, self.recv, self.prior, self.fin = send, recv, prior, fin
        self.send_sem, self.recv_sem = send_sem, recv_sem
        self.half = state.shape[0] // 2
        self.core = lax.rem(seq, 2)
        self.mine = pl.ds(pl.multiple_of(self.core * self.half, 16), self.half)
        self.other = pl.ds(pl.multiple_of((1 - self.core) * self.half, 16), self.half)
        self.at = 0
        self.copies = []

    def bit(self, step):
        return lax.rem(self.seq // (1 << step), 2)

    def partner(self, step):
        return self.seq + (1 - 2 * self.bit(step)) * (1 << step)

    def push(self, src, dst, index, step):
        copy = pltpu.make_async_remote_copy(
            src_ref=src,
            dst_ref=dst,
            send_sem=self.send_sem.at[index],
            recv_sem=self.recv_sem.at[index],
            device_id={"seq": self.partner(step)},
            device_id_type=MESH,
        )
        copy.start()
        self.copies.append(copy)

    def begin(self):
        self.send[0] = self.state[self.other, :].astype(BF16)
        self.push(self.send.at[0], self.recv.at[0], 0, 0)

    def advance(self):
        step = self.at
        if step > self.steps:
            return
        self.at += 1
        self.copies[step].wait_recv()
        if step == self.steps:
            return
        came = self.recv[step].astype(F32)
        if step == 0:
            self.total[...] = self.state[self.mine, :] + came
            self.before[...] = jnp.zeros(self.before.shape, F32)
        else:
            self.before[...] += jnp.where(self.bit(step) == 1, came, 0.0)
            if step < self.steps - 1:
                self.total[...] += came
        if step < self.steps - 1:
            self.send[step + 1] = self.total[...].astype(BF16)
            self.push(self.send.at[step + 1], self.recv.at[step + 1], step + 1, step + 1)
        else:
            before = self.before[...]
            first = self.recv[0].astype(F32)
            extra = jnp.where(self.core == 0, self.state[self.mine, :], 0.0)
            self.fin[...] = (before + extra).astype(BF16)
            self.push(self.fin, self.prior.at[self.mine, :], self.steps, 0)
            self.prior[self.mine, :] = (before + jnp.where(self.core == 1, first, 0.0)).astype(BF16)

    def drain(self):
        while self.at <= self.steps:
            self.advance()

    def close(self):
        for copy in self.copies:
            copy.wait_send()


def kernel(
    n, steps, sub,
    tok_hbm, wq_hbm, wk_hbm, wv_hbm, wo_hbm, gain_ref, out_ref,
    tok, own, own_o, wide, wide_o, kvq, within, normed, acc,
    state_a, total_a, before_a, send_a, recv_a, prior_a, fin_a,
    state_b, total_b, before_b, send_b, recv_b, prior_b, fin_b,
    load_sem, y_send, y_recv, x_send, x_recv, c_send, c_recv, d_send, d_recv,
    as_send, as_recv, bs_send, bs_recv,
):
    dp, seq = lax.axis_index("dp"), lax.axis_index("seq")
    length, width = tok.shape
    cols = own.shape[2]
    heads = cols // DH
    sources = [wk_hbm, wv_hbm, wq_hbm, wo_hbm]
    rank = lax.rem(seq, GROUP)
    core = lax.rem(seq, 2)
    xbit = lax.rem(seq // 2, 2)
    core_mate = seq + 1 - 2 * core
    x_mate = seq + 2 * (1 - 2 * xbit)
    x_rank = rank + 2 * (1 - 2 * xbit)

    loads = [pltpu.make_async_copy(tok_hbm, tok, load_sem.at[4])]
    for kind in range(4):
        dst = own.at[kind] if kind < 3 else own_o
        loads.append(pltpu.make_async_copy(sources[kind], dst, load_sem.at[kind]))
    for copy in loads:
        copy.start()

    barrier = pltpu.get_barrier_semaphore()
    for slot in range(1, n):
        pl.semaphore_signal(barrier, inc=1, device_id={"dp": lax.rem(dp + slot, n)}, device_id_type=MESH)
    for step in range(steps):
        bit = lax.rem(seq // (1 << step), 2)
        mate = seq + (1 - 2 * bit) * (1 << step)
        pl.semaphore_signal(barrier, inc=1, device_id={"seq": mate}, device_id_type=MESH)
    pl.semaphore_wait(barrier, n - 1 + steps)

    def rows_of(kind, who, s):
        quarter = sources[kind].shape[0] // GROUP
        size = quarter // sub
        return pl.ds(pl.multiple_of(who * quarter + s * size, 16), size)

    def place(kind, slot, rows):
        if kind < 3:
            return wide.at[slot - 1, kind, rows, :]
        return wide_o.at[slot - 1, rows, :]

    pieces = [[(kind, slot, s) for s in range(sub) for slot in range(1, n)] for kind in range(4)]
    remote, sent = {}, []

    def push(src, dst, send, recv, target):
        copy = pltpu.make_async_remote_copy(
            src_ref=src, dst_ref=dst, send_sem=send, recv_sem=recv, device_id=target, device_id_type=MESH
        )
        copy.start()
        sent.append(copy)
        return copy

    for kind in range(4):
        for piece in pieces[kind]:
            _, slot, s = piece
            index = (kind, slot - 1, s)
            rows = rows_of(kind, rank, s)
            remote["y", piece] = push(
                sources[kind].at[rows, :], place(kind, slot, rows), y_send.at[index], y_recv.at[index],
                {"dp": lax.rem(dp - slot + n, n)},
            )

    def relay(piece):
        kind, slot, s = piece
        index = (kind, slot - 1, s)
        here = place(kind, slot, rows_of(kind, rank, s))
        remote["y", piece].wait_recv()
        remote["x", piece] = push(here, here, x_send.at[index], x_recv.at[index], {"seq": x_mate})
        remote["c", piece] = push(here, here, c_send.at[index], c_recv.at[index], {"seq": core_mate})

    def relay_again(piece):
        kind, slot, s = piece
        index = (kind, slot - 1, s)
        here = place(kind, slot, rows_of(kind, x_rank, s))
        remote["x", piece].wait_recv()
        remote["d", piece] = push(here, here, d_send.at[index], d_recv.at[index], {"seq": core_mate})

    order = [piece for kind in range(4) for piece in pieces[kind]]
    half_of = len(pieces[0]) // 2 or 1
    cuts = []
    for kind in range(4):
        base = kind * len(pieces[0])
        cuts.append(base + half_of)
        cuts.append(base + len(pieces[0]))
    done = {"first": 0, "again": 0}

    def pump(first, again):
        first = cuts[first - 1] if first else 0
        again = cuts[again - 1] if again else 0
        while done["first"] < first or done["again"] < again:
            if done["again"] < again and done["again"] < done["first"] - 1 or done["first"] >= first:
                relay_again(order[done["again"]])
                done["again"] += 1
            else:
                relay(order[done["first"]])
                done["first"] += 1

    def ready(kind):
        for piece in pieces[kind]:
            remote["c", piece].wait_recv()
            remote["d", piece].wait_recv()

    chunk = min(256, cols)

    def project(kind, slot):
        source = own.at[kind] if slot == 0 else wide.at[slot - 1, kind]

        @pl.loop(0, cols // chunk)
        def _(i):
            at = pl.ds(pl.multiple_of(i * chunk, 128), chunk)
            kvq[kind, slot, :, at] = jnp.dot(tok[...], source[:, at], preferred_element_type=F32).astype(BF16)

    def states(slot, ref, base):
        @pl.loop(0, heads)
        def _(h):
            at = pl.ds(pl.multiple_of(h * DH, DH), DH)
            ref[pl.ds(pl.multiple_of(base + h * DH, DH), DH), :] = lax.dot_general(
                kvq[0, slot, :, at], kvq[1, slot, :, at], (((0,), (0,)), ((), ())), preferred_element_type=F32
            )

    half = length // 2

    def inner(slot):
        @pl.loop(0, heads)
        def _(h):
            at = pl.ds(pl.multiple_of(h * DH, DH), DH)
            for begin in (0, half):
                end = begin + half
                scores = lax.dot_general(
                    kvq[2, slot, begin:end, at], kvq[0, slot, :end, at], (((1,), (1,)), ((), ())),
                    preferred_element_type=F32,
                )
                row = begin + lax.broadcasted_iota(jnp.int32, (half, end), 0)
                col = lax.broadcasted_iota(jnp.int32, (half, end), 1)
                scores = jnp.where(col <= row, scores, 0.0).astype(BF16)
                within[slot, begin:end, at] = jnp.dot(
                    scores, kvq[1, slot, :end, at], preferred_element_type=F32
                )

    def finish(slot, prior, base):
        owner = lax.rem(dp + slot, n)

        @pl.loop(0, heads)
        def _(h):
            at = pl.ds(pl.multiple_of(h * DH, DH), DH)
            carried = jnp.dot(
                kvq[2, slot, :, at], prior[pl.ds(pl.multiple_of(base + h * DH, DH), DH), :],
                preferred_element_type=F32,
            )
            mixed = within[slot, :, at] + carried
            scale = lax.rsqrt(jnp.sum(mixed * mixed, axis=-1, keepdims=True) * (1.0 / DH) + 1e-05)
            normed[slot, :, at] = (mixed * scale * gain_ref[pl.ds(owner * heads + h, 1), :]).astype(BF16)

    def join(slot):
        source = own_o if slot == 0 else wide_o.at[slot - 1]

        @pl.loop(0, width // 256)
        def _(i):
            at = pl.ds(pl.multiple_of(i * 256, 128), 256)
            part = jnp.dot(normed[slot], source[:, at], preferred_element_type=F32)
            if slot > 0:
                part = acc[:, at] + part
            if slot == n - 1:
                out_ref[:, at] = part.astype(BF16)
            else:
                acc[:, at] = part

    scan_a = Scan(seq, steps, state_a, total_a, before_a, send_a, recv_a, prior_a, fin_a, as_send, as_recv)
    scan_b = Scan(seq, steps, state_b, total_b, before_b, send_b, recv_b, prior_b, fin_b, bs_send, bs_recv)

    loads[0].wait()
    loads[1].wait()
    project(0, 0)
    loads[2].wait()
    project(1, 0)
    states(0, state_a, 0)
    scan_a.begin()
    pump(1, 0)
    loads[3].wait()
    project(2, 0)
    pump(2, 1)
    scan_a.advance()
    inner(0)
    pump(3, 2)
    scan_a.advance()
    ready(0)
    for slot in range(1, n):
        project(0, slot)
    pump(4, 3)
    scan_a.advance()
    pump(4, 4)
    ready(1)
    for slot in range(1, n):
        project(1, slot)
        states(slot, state_b, (slot - 1) * cols)
    scan_b.begin()
    scan_a.advance()
    pump(5, 4)
    scan_b.advance()
    scan_a.drain()
    finish(0, prior_a, 0)
    pump(6, 5)
    scan_b.advance()
    loads[4].wait()
    join(0)
    pump(7, 6)
    scan_b.advance()
    ready(2)
    for slot in range(1, n):
        project(2, slot)
        inner(slot)
    pump(8, 7)
    scan_b.advance()
    scan_b.drain()
    for slot in range(1, n):
        finish(slot, prior_b, (slot - 1) * cols)
    pump(8, 8)
    ready(3)
    for slot in range(1, n):
        join(slot)
    for copy in sent:
        copy.wait_send()
    scan_a.close()
    scan_b.close()


def body(n, seqs, tokens, w_query, w_key, w_value, w_out, norm_gain):
    length, width = tokens.shape[1:]
    cols = w_query.shape[1]
    depth = w_out.shape[0]
    steps = seqs.bit_length() - 1
    sub = 2 if n <= 2 else 1
    any_spec = pl.BlockSpec(memory_space=pl.ANY)
    vmem = pl.BlockSpec(memory_space=pltpu.VMEM)
    scans = []
    for rows in (cols, (n - 1) * cols):
        part = rows // 2
        scans += [
            pltpu.VMEM((rows, DH), F32),
            pltpu.VMEM((part, DH), F32),
            pltpu.VMEM((part, DH), F32),
            pltpu.VMEM((steps, part, DH), BF16),
            pltpu.VMEM((steps, part, DH), BF16),
            pltpu.VMEM((rows, DH), BF16),
            pltpu.VMEM((part, DH), BF16),
        ]
    out = pl.pallas_call(
        functools.partial(kernel, n, steps, sub),
        out_shape=jax.ShapeDtypeStruct((length, width), BF16),
        in_specs=[any_spec] * 5 + [vmem],
        out_specs=vmem,
        scratch_shapes=[
            pltpu.VMEM((length, width), BF16),
            pltpu.VMEM((3, width, cols), BF16),
            pltpu.VMEM((depth, width), BF16),
            pltpu.VMEM((n - 1, 3, width, cols), BF16),
            pltpu.VMEM((n - 1, depth, width), BF16),
            pltpu.VMEM((3, n, length, cols), BF16),
            pltpu.VMEM((n, length, cols), F32),
            pltpu.VMEM((n, length, cols), BF16),
            pltpu.VMEM((length, width), F32),
        ]
        + scans
        + [pltpu.SemaphoreType.DMA((5,))]
        + [pltpu.SemaphoreType.DMA((4, n - 1, sub))] * 8
        + [pltpu.SemaphoreType.DMA((steps + 1,))] * 4,
        compiler_params=pltpu.CompilerParams(
            collective_id=0, has_side_effects=True, vmem_limit_bytes=50 * 1024 * 1024
        ),
    )(tokens[0], w_query, w_key, w_value, w_out, norm_gain.reshape(-1, DH))
    return out[None]


def solution(mesh):
    in_specs = (
        P("dp", "seq", None),
        P(None, "dp"),
        P(None, "dp"),
        P(None, "dp"),
        P("dp", None),
        P(),
    )
    out_specs = P("dp", "seq", None)
    fn = functools.partial(body, mesh.shape["dp"], mesh.shape["seq"])
    return jax.shard_map(fn, mesh=mesh, in_specs=in_specs, out_specs=out_specs, check_vma=False)
```

time: 203 us -> 53.8 us (0.27)
  waiting for transfers between devices: 158 us -> 0 us
  Pallas kernels: 0 us -> 49.4 us
  matrix products: 18.7 us -> 0 us
  between operations: 13.2 us -> 0.01 us
  local copies, waits for them, and re-layouts: 9.22 us -> 4.11 us
  other arithmetic: 3.68 us -> 0 us
    all_gather x3 -> x0, waiting for transfers between devices: 157 us -> none  [the longest x1 83.2 us: body(): lax.all_gather(stacked, 'dp', axis=2, tiled=True)]
    pallas_call x0 -> x1, Pallas kernels: none -> 49.4 us  [body(): pl.pallas_call(functools.partial(kernel, n, steps, sub), out_shape=jax.Sh...]
    dot_general x5 -> x0, matrix products: 18.7 us -> none  [the longest x1 6.49 us: body(): jnp.einsum('td,pdc->ptc', rows, lax.all_gather(stacked, 'dp', axis=2, til...]
    another operation x1 -> x0, other arithmetic: 3.27 us -> none  [body(): stacked = jnp.stack([w_query, w_key, w_value], axis=0)]
    unnamed x9 -> x7, local copies, waits for them, and re-layouts: 6.4 us -> 4.11 us
  transfers between devices with their start and end apart: 3 -> 0, of which waited for: 3 -> 0; matrix products, arithmetic and copies ran while one was open for 5% -> 0% of each run, Pallas kernels for 0% -> 0%
where the time goes in v1:
time: 53.8 us; the launch traced here: 53.5 us
  Pallas kernels  49.4 us (92%)
  local copies, waits for them, and re-layouts  4.11 us (8%)
    pallas_call x1, Pallas kernels, body(): pl.pallas_call(functools.partial(kernel, n, steps, sub), out_shape=jax.Sh...  49.4 us
    unnamed x7, local copies, waits for them, and re-layouts  4.11 us

profile of v1, /device:TPU:0, one launch (start us, length us, event | category | flops | bytes accessed | tf_op | source)
XLA Modules:
  0.0 53.5 jit_solution(8738678220776674343)
XLA Ops:
  0.0 0.0 copy-start
  0.0 1.2 %copy-done = bf16[1,512,1024]{2,1,0:T(8,128)(2,1)S(1)} copy-done((bf16[1,512,1024]{2,1,0:T(8,128)(2,1)S(1)}, bf16[1,512,1024]{2,1,0:T(8,128)(2,1)}, u32[]{:S(2)}) %copy-start) | copy-done | bytes 1048600
  1.2 0.0 copy-start.1
  1.2 1.2 %copy-done.1 = bf16[1024,512]{1,0:T(8,128)(2,1)S(1)} copy-done((bf16[1024,512]{1,0:T(8,128)(2,1)S(1)}, bf16[1024,512]{1,0:T(8,128)(2,1)}, u32[]{:S(2)}) %copy-start.1) | copy-done | bytes 1048600
  2.5 0.0 copy-start.2
  2.5 0.7 %copy-done.2 = f32[1024]{0:T(1024)S(1)} copy-done((f32[1024]{0:T(1024)S(1)}, f32[1024]{0:T(1024)}, u32[]{:S(2)}) %copy-start.2) | copy-done | bytes 4120
  3.1 49.4 %shard_map.64 = bf16[512,1024]{1,0:T(8,128)(2,1)S(1)} custom-call(bf16[512,1024]{1,0:T(8,128)(2,1)S(1)} %bitcast.4, bf16[1024,512]{1,0:T(8,128)(2,1)S(1)} %copy-done.1, bf16[1024,512]{1,0:T(8,128)(2,1)} %wk_hbm.1, bf16[1024,512]{1,0:T(8,128)(2,1)} %wv_hbm.1, bf16[512,1024]{1,0:T(8,128)(2,1)} %wo_hbm.1, f32[8,128]{1,0:T(8,128)S(1)} %bitcast.5), custom_call_target="tpu_custom_call" | custom-call | tf_op jit(solution)/shard_map/pallas_call | solution.py:341
  52.6 1.0 %copy.8 = bf16[1,512,1024]{2,1,0:T(8,128)(2,1)} copy(bf16[1,512,1024]{2,1,0:T(8,128)(2,1)S(1)} %bitcast.3) | data formatting | bytes 2097152
Async XLA Ops:
  0.0 1.2 %copy-start = (bf16[1,512,1024]{2,1,0:T(8,128)(2,1)S(1)}, bf16[1,512,1024]{2,1,0:T(8,128)(2,1)}, u32[]{:S(2)}) copy-start(bf16[1,512,1024]{2,1,0:T(8,128)(2,1)} %param.6) | copy-start | bytes 3145732
  1.2 1.2 %copy-start.1 = (bf16[1024,512]{1,0:T(8,128)(2,1)S(1)}, bf16[1024,512]{1,0:T(8,128)(2,1)}, u32[]{:S(2)}) copy-start(bf16[1024,512]{1,0:T(8,128)(2,1)} %wq_hbm.1) | copy-start | bytes 3145732
  2.5 0.7 %copy-start.2 = (f32[1024]{0:T(1024)S(1)}, f32[1024]{0:T(1024)}, u32[]{:S(2)}) copy-start(f32[1024]{0:T(1024)} %param.11) | copy-start | bytes 12292

commit v2 on v1

--- a/solution.py
+++ b/solution.py
@@ -9,7 +9,7 @@
 
 H = 8
 DH = 128
-GROUP = 4
+GROUP = 8
 MESH = pl.DeviceIdType.MESH
 F32 = jnp.float32
 BF16 = jnp.bfloat16
@@ -92,7 +92,7 @@
     tok, own, own_o, wide, wide_o, kvq, within, normed, acc,
     state_a, total_a, before_a, send_a, recv_a, prior_a, fin_a,
     state_b, total_b, before_b, send_b, recv_b, prior_b, fin_b,
-    load_sem, y_send, y_recv, x_send, x_recv, c_send, c_recv, d_send, d_recv,
+    load_sem, sends, recvs,
     as_send, as_recv, bs_send, bs_recv,
 ):
     dp, seq = lax.axis_index("dp"), lax.axis_index("seq")
@@ -105,7 +105,12 @@
     xbit = lax.rem(seq // 2, 2)
     core_mate = seq + 1 - 2 * core
     x_mate = seq + 2 * (1 - 2 * xbit)
+    zbit = lax.rem(seq // 4, 2)
+    z_mate = seq + 4 * (1 - 2 * zbit)
     x_rank = rank + 2 * (1 - 2 * xbit)
+    z_rank = rank + 4 * (1 - 2 * zbit)
+    g_rank = z_rank + 2 * (1 - 2 * xbit)
+    lanes = ("y", "x", "z", "g", "c0", "c1", "c2", "c3")
 
     loads = [pltpu.make_async_copy(tok_hbm, tok, load_sem.at[4])]
     for kind in range(4):
@@ -147,52 +152,61 @@
     for kind in range(4):
         for piece in pieces[kind]:
             _, slot, s = piece
-            index = (kind, slot - 1, s)
+            index = (0, kind, slot - 1, s)
             rows = rows_of(kind, rank, s)
             remote["y", piece] = push(
-                sources[kind].at[rows, :], place(kind, slot, rows), y_send.at[index], y_recv.at[index],
+                sources[kind].at[rows, :], place(kind, slot, rows), sends.at[index], recvs.at[index],
                 {"dp": lax.rem(dp - slot + n, n)},
             )
 
+    def forward(name, piece, who, target):
+        kind, slot, s = piece
+        here = place(kind, slot, rows_of(kind, who, s))
+        index = (lanes.index(name), kind, slot - 1, s)
+        remote[name, piece] = push(here, here, sends.at[index], recvs.at[index], target)
+
     def relay(piece):
-        kind, slot, s = piece
-        index = (kind, slot - 1, s)
-        here = place(kind, slot, rows_of(kind, rank, s))
         remote["y", piece].wait_recv()
-        remote["x", piece] = push(here, here, x_send.at[index], x_recv.at[index], {"seq": x_mate})
-        remote["c", piece] = push(here, here, c_send.at[index], c_recv.at[index], {"seq": core_mate})
+        forward("x", piece, rank, {"seq": x_mate})
+        forward("z", piece, rank, {"seq": z_mate})
+        forward("c0", piece, rank, {"seq": core_mate})
 
     def relay_again(piece):
-        kind, slot, s = piece
-        index = (kind, slot - 1, s)
-        here = place(kind, slot, rows_of(kind, x_rank, s))
+        even = (piece[1] + piece[2]) % 2 == 1
         remote["x", piece].wait_recv()
-        remote["d", piece] = push(here, here, d_send.at[index], d_recv.at[index], {"seq": core_mate})
+        if even:
+            forward("g", piece, x_rank, {"seq": z_mate})
+        forward("c1", piece, x_rank, {"seq": core_mate})
+        remote["z", piece].wait_recv()
+        if not even:
+            forward("g", piece, z_rank, {"seq": x_mate})
+        forward("c2", piece, z_rank, {"seq": core_mate})
+
+    def relay_last(piece):
+        remote["g", piece].wait_recv()
+        forward("c3", piece, g_rank, {"seq": core_mate})
 
     order = [piece for kind in range(4) for piece in pieces[kind]]
     half_of = len(pieces[0]) // 2 or 1
-    cuts = []
+    cuts = [0]
     for kind in range(4):
         base = kind * len(pieces[0])
-        cuts.append(base + half_of)
-        cuts.append(base + len(pieces[0]))
-    done = {"first": 0, "again": 0}
-
-    def pump(first, again):
-        first = cuts[first - 1] if first else 0
-        again = cuts[again - 1] if again else 0
-        while done["first"] < first or done["again"] < again:
-            if done["again"] < again and done["again"] < done["first"] - 1 or done["first"] >= first:
-                relay_again(order[done["again"]])
-                done["again"] += 1
-            else:
-                relay(order[done["first"]])
-                done["first"] += 1
+        cuts += [base + half_of, base + len(pieces[0])]
+    acts = (relay, relay_again, relay_last)
+    done = [0, 0, 0]
+
+    def pump(*goals):
+        goals = [cuts[goal] for goal in goals]
+        while any(at < goal for at, goal in zip(done, goals)):
+            todo = [i for i in range(3) if done[i] < goals[i] and (i == 0 or done[i] < done[i - 1])]
+            pick = min(todo, key=lambda i: (done[i] + i, -i))
+            acts[pick](order[done[pick]])
+            done[pick] += 1
 
     def ready(kind):
         for piece in pieces[kind]:
-            remote["c", piece].wait_recv()
-            remote["d", piece].wait_recv()
+            for name in ("c0", "c1", "c2", "c3"):
+                remote[name, piece].wait_recv()
 
     chunk = min(256, cols)
 
@@ -262,55 +276,58 @@
     scan_a = Scan(seq, steps, state_a, total_a, before_a, send_a, recv_a, prior_a, fin_a, as_send, as_recv)
     scan_b = Scan(seq, steps, state_b, total_b, before_b, send_b, recv_b, prior_b, fin_b, bs_send, bs_recv)
 
+    others = range(1, n)
     loads[0].wait()
     loads[1].wait()
     project(0, 0)
+    pump(1, 0, 0)
     loads[2].wait()
     project(1, 0)
     states(0, state_a, 0)
     scan_a.begin()
-    pump(1, 0)
+    pump(2, 1, 0)
     loads[3].wait()
     project(2, 0)
-    pump(2, 1)
+    pump(3, 2, 1)
     scan_a.advance()
     inner(0)
-    pump(3, 2)
+    pump(4, 3, 2)
     scan_a.advance()
     ready(0)
-    for slot in range(1, n):
+    for slot in others:
         project(0, slot)
-    pump(4, 3)
+    pump(5, 4, 3)
     scan_a.advance()
-    pump(4, 4)
+    pump(5, 5, 4)
     ready(1)
-    for slot in range(1, n):
+    for slot in others:
         project(1, slot)
         states(slot, state_b, (slot - 1) * cols)
     scan_b.begin()
     scan_a.advance()
-    pump(5, 4)
+    pump(6, 5, 5)
     scan_b.advance()
     scan_a.drain()
     finish(0, prior_a, 0)
-    pump(6, 5)
+    pump(7, 6, 5)
     scan_b.advance()
     loads[4].wait()
     join(0)
-    pump(7, 6)
+    pump(8, 7, 6)
     scan_b.advance()
     ready(2)
-    for slot in range(1, n):
+    for slot in others:
         project(2, slot)
+    pump(8, 8, 7)
+    scan_b.advance()
+    for slot in others:
         inner(slot)
-    pump(8, 7)
-    scan_b.advance()
+    pump(8, 8, 8)
     scan_b.drain()
-    for slot in range(1, n):
+    for slot in others:
         finish(slot, prior_b, (slot - 1) * cols)
-    pump(8, 8)
     ready(3)
-    for slot in range(1, n):
+    for slot in others:
         join(slot)
     for copy in sent:
         copy.wait_send()
@@ -356,10 +373,10 @@
         ]
         + scans
         + [pltpu.SemaphoreType.DMA((5,))]
-        + [pltpu.SemaphoreType.DMA((4, n - 1, sub))] * 8
+        + [pltpu.SemaphoreType.DMA((8, 4, n - 1, sub))] * 2
         + [pltpu.SemaphoreType.DMA((steps + 1,))] * 4,
         compiler_params=pltpu.CompilerParams(
-            collective_id=0, has_side_effects=True, vmem_limit_bytes=50 * 1024 * 1024
+            collective_id=0, has_side_effects=True, vmem_limit_bytes=67043328
         ),
     )(tokens[0], w_query, w_key, w_value, w_out, norm_gain.reshape(-1, DH))
     return out[None]

time: 53.8 us -> 57.8 us (1.074)
  Pallas kernels: 49.4 us -> 55.4 us
  local copies, waits for them, and re-layouts: 4.11 us -> 2.26 us
    pallas_call x1, Pallas kernels: 49.4 us -> 55.4 us  [body(): pl.pallas_call(functools.partial(kernel, n, steps, sub), out_shape=jax.Sh...]
    unnamed x7 -> x1, local copies, waits for them, and re-layouts: 4.11 us -> 2.26 us
where the time goes in v2:
time: 57.8 us; the launch traced here: 57.6 us
  Pallas kernels  55.4 us (96%)
  local copies, waits for them, and re-layouts  2.26 us (4%)
    pallas_call x1, Pallas kernels, body(): pl.pallas_call(functools.partial(kernel, n, steps, sub), out_shape=jax.Sh...  55.4 us
    unnamed x1, local copies, waits for them, and re-layouts  2.26 us

profile of v2, /device:TPU:0, one launch (start us, length us, event | category | flops | bytes accessed | tf_op | source)
XLA Modules:
  0.0 57.6 jit_solution(12788283364312179926)
XLA Ops:
  0.0 55.4 %shard_map.64 = bf16[512,1024]{1,0:T(8,128)(2,1)} custom-call(bf16[512,1024]{1,0:T(8,128)(2,1)} %bitcast.4, bf16[1024,512]{1,0:T(8,128)(2,1)} %wq_hbm.1, bf16[1024,512]{1,0:T(8,128)(2,1)} %wk_hbm.1, bf16[1024,512]{1,0:T(8,128)(2,1)} %wv_hbm.1, bf16[512,1024]{1,0:T(8,128)(2,1)} %wo_hbm.1, f32[8,128]{1,0:T(8,128)} %bitcast.5), custom_call_target="tpu_custom_call" | custom-call | tf_op jit(solution)/shard_map/pallas_call | solution.py:358
  55.4 2.3 %copy.8 = bf16[1,512,1024]{2,1,0:T(8,128)(2,1)} copy(bf16[1,512,1024]{2,1,0:T(8,128)(2,1)} %bitcast.3) | data formatting | bytes 2097152

commit v3 on v2

--- a/solution.py
+++ b/solution.py
@@ -199,7 +199,7 @@
         goals = [cuts[goal] for goal in goals]
         while any(at < goal for at, goal in zip(done, goals)):
             todo = [i for i in range(3) if done[i] < goals[i] and (i == 0 or done[i] < done[i - 1])]
-            pick = min(todo, key=lambda i: (done[i] + i, -i))
+            pick = min(todo, key=lambda i: done[i] + 2 * half_of * i)
             acts[pick](order[done[pick]])
             done[pick] += 1
 
@@ -283,37 +283,38 @@
     pump(1, 0, 0)
     loads[2].wait()
     project(1, 0)
+    pump(2, 0, 0)
     states(0, state_a, 0)
     scan_a.begin()
-    pump(2, 1, 0)
+    pump(3, 0, 0)
     loads[3].wait()
     project(2, 0)
-    pump(3, 2, 1)
+    pump(4, 1, 0)
     scan_a.advance()
     inner(0)
-    pump(4, 3, 2)
+    pump(5, 3, 1)
     scan_a.advance()
+    pump(6, 4, 2)
     ready(0)
     for slot in others:
         project(0, slot)
-    pump(5, 4, 3)
+    pump(7, 5, 3)
     scan_a.advance()
-    pump(5, 5, 4)
+    pump(8, 6, 4)
     ready(1)
     for slot in others:
         project(1, slot)
         states(slot, state_b, (slot - 1) * cols)
     scan_b.begin()
     scan_a.advance()
-    pump(6, 5, 5)
+    pump(8, 7, 5)
     scan_b.advance()
     scan_a.drain()
     finish(0, prior_a, 0)
-    pump(7, 6, 5)
     scan_b.advance()
+    pump(8, 8, 6)
     loads[4].wait()
     join(0)
-    pump(8, 7, 6)
     scan_b.advance()
     ready(2)
     for slot in others:

time: 57.8 us -> 49.5 us (0.86)
  Pallas kernels: 55.4 us -> 47 us
    pallas_call x1, Pallas kernels: 55.4 us -> 47 us  [body(): pl.pallas_call(functools.partial(kernel, n, steps, sub), out_shape=jax.Sh...]
where the time goes in v3:
time: 49.5 us; the launch traced here: 49.3 us
  Pallas kernels  47 us (95%)
  local copies, waits for them, and re-layouts  2.26 us (5%)
    pallas_call x1, Pallas kernels, body(): pl.pallas_call(functools.partial(kernel, n, steps, sub), out_shape=jax.Sh...  47 us
    unnamed x1, local copies, waits for them, and re-layouts  2.26 us

profile of v3, /device:TPU:0, one launch (start us, length us, event | category | flops | bytes accessed | tf_op | source)
XLA Modules:
  0.0 49.3 jit_solution(17515741461566683069)
XLA Ops:
  0.0 47.0 %shard_map.64 = bf16[512,1024]{1,0:T(8,128)(2,1)} custom-call(bf16[512,1024]{1,0:T(8,128)(2,1)} %bitcast.4, bf16[1024,512]{1,0:T(8,128)(2,1)} %wq_hbm.1, bf16[1024,512]{1,0:T(8,128)(2,1)} %wk_hbm.1, bf16[1024,512]{1,0:T(8,128)(2,1)} %wv_hbm.1, bf16[512,1024]{1,0:T(8,128)(2,1)} %wo_hbm.1, f32[8,128]{1,0:T(8,128)} %bitcast.5), custom_call_target="tpu_custom_call" | custom-call | tf_op jit(solution)/shard_map/pallas_call | solution.py:359
  47.1 2.3 %copy.8 = bf16[1,512,1024]{2,1,0:T(8,128)(2,1)} copy(bf16[1,512,1024]{2,1,0:T(8,128)(2,1)} %bitcast.3) | data formatting | bytes 2097152

commit v4 on v3

--- a/solution.py
+++ b/solution.py
@@ -10,6 +10,7 @@
 H = 8
 DH = 128
 GROUP = 8
+DIRECT = ((3, 1),)
 MESH = pl.DeviceIdType.MESH
 F32 = jnp.float32
 BF16 = jnp.bfloat16
@@ -128,10 +129,13 @@
         pl.semaphore_signal(barrier, inc=1, device_id={"seq": mate}, device_id_type=MESH)
     pl.semaphore_wait(barrier, n - 1 + steps)
 
+    def direct(kind, s):
+        return (kind, s) in DIRECT
+
     def rows_of(kind, who, s):
-        quarter = sources[kind].shape[0] // GROUP
-        size = quarter // sub
-        return pl.ds(pl.multiple_of(who * quarter + s * size, 16), size)
+        region = sources[kind].shape[0] // sub
+        size = region // (2 if direct(kind, s) else GROUP)
+        return pl.ds(pl.multiple_of(s * region + who * size, 16), size)
 
     def place(kind, slot, rows):
         if kind < 3:
@@ -153,7 +157,7 @@
         for piece in pieces[kind]:
             _, slot, s = piece
             index = (0, kind, slot - 1, s)
-            rows = rows_of(kind, rank, s)
+            rows = rows_of(kind, core if direct(kind, s) else rank, s)
             remote["y", piece] = push(
                 sources[kind].at[rows, :], place(kind, slot, rows), sends.at[index], recvs.at[index],
                 {"dp": lax.rem(dp - slot + n, n)},
@@ -167,11 +171,16 @@
 
     def relay(piece):
         remote["y", piece].wait_recv()
+        if direct(piece[0], piece[2]):
+            forward("c0", piece, core, {"seq": core_mate})
+            return
         forward("x", piece, rank, {"seq": x_mate})
         forward("z", piece, rank, {"seq": z_mate})
         forward("c0", piece, rank, {"seq": core_mate})
 
     def relay_again(piece):
+        if direct(piece[0], piece[2]):
+            return
         even = (piece[1] + piece[2]) % 2 == 1
         remote["x", piece].wait_recv()
         if even:
@@ -183,6 +192,8 @@
         forward("c2", piece, z_rank, {"seq": core_mate})
 
     def relay_last(piece):
+        if direct(piece[0], piece[2]):
+            return
         remote["g", piece].wait_recv()
         forward("c3", piece, g_rank, {"seq": core_mate})
 
@@ -205,7 +216,7 @@
 
     def ready(kind):
         for piece in pieces[kind]:
-            for name in ("c0", "c1", "c2", "c3"):
+            for name in ("c0",) if direct(kind, piece[2]) else ("c0", "c1", "c2", "c3"):
                 remote[name, piece].wait_recv()
 
     chunk = min(256, cols)

time: 49.5 us -> 47.7 us (0.964)
  Pallas kernels: 47 us -> 45.3 us
    pallas_call x1, Pallas kernels: 47 us -> 45.3 us  [body(): pl.pallas_call(functools.partial(kernel, n, steps, sub), out_shape=jax.Sh...]
where the time goes in v4:
time: 47.7 us; the launch traced here: 47.5 us
  Pallas kernels  45.3 us (95%)
  local copies, waits for them, and re-layouts  2.26 us (5%)
    pallas_call x1, Pallas kernels, body(): pl.pallas_call(functools.partial(kernel, n, steps, sub), out_shape=jax.Sh...  45.3 us
    unnamed x1, local copies, waits for them, and re-layouts  2.26 us

profile of v4, /device:TPU:0, one launch (start us, length us, event | category | flops | bytes accessed | tf_op | source)
XLA Modules:
  0.0 47.5 jit_solution(14543722335343991412)
XLA Ops:
  0.0 45.3 %shard_map.64 = bf16[512,1024]{1,0:T(8,128)(2,1)} custom-call(bf16[512,1024]{1,0:T(8,128)(2,1)} %bitcast.4, bf16[1024,512]{1,0:T(8,128)(2,1)} %wq_hbm.1, bf16[1024,512]{1,0:T(8,128)(2,1)} %wk_hbm.1, bf16[1024,512]{1,0:T(8,128)(2,1)} %wv_hbm.1, bf16[512,1024]{1,0:T(8,128)(2,1)} %wo_hbm.1, f32[8,128]{1,0:T(8,128)} %bitcast.5), custom_call_target="tpu_custom_call" | custom-call | tf_op jit(solution)/shard_map/pallas_call | solution.py:370
  45.3 2.3 %copy.8 = bf16[1,512,1024]{2,1,0:T(8,128)(2,1)} copy(bf16[1,512,1024]{2,1,0:T(8,128)(2,1)} %bitcast.3) | data formatting | bytes 2097152
